TPU v7x, 512 devices: a whole 4x4x16 slice. The times are simulated.
512 devices in a mesh: tm: 16 (over z_hi, y), pipe: 2 (over core), dp: 16 (over x, z_lo).
Axes of the slice: x: 4, y: 4, z: 16 (z_hi: 4, z_lo: 4; z = z_hi * 4 + z_lo), core: 2. Of those that a mesh axis runs over, the one named last changes fastest.
Arguments:
- resid_in: float32 [2, 96, 1024, 1408], P('pipe', 'dp', 'tm'), may hold values from -6 to 6
- ln_gain: float32 [2, 1408], P('pipe'), may hold values from 0.5 to 1.5
- ln_bias: float32 [2, 1408], P('pipe'), may hold values from -2 to 2
- qkv_weight: bfloat16 [2, 1408, 2112], P('pipe', None, 'dp'), may hold values from -0.15625 to 0.15625
- q_bias: float32 [2, 704], P('pipe'), may hold values from -3 to 3
- v_bias: float32 [2, 704], P('pipe'), may hold values from -3 to 3
- out_weight: bfloat16 [2, 1408, 704], P('pipe', None, 'dp'), may hold values from -0.21875 to 0.21875
- out_bias: float32 [2, 1408], P('pipe'), may hold values from -2 to 2
- pattern: int32 [16, 96, 2], P('tm', 'dp'), may hold values from 0 to 14, all different within a row; in each aligned block of 6 rows (0 to 5, 6 to 11, ..., all dimensions but the last counted through in order) at most 2 rows name the same one
- drop_flags: int32 [2, 96], P('pipe', 'dp'), may hold values 0 or 1
Outputs:
- handoff: float32 [2, 96, 1024, 1408], P('pipe', 'dp', 'tm')
Inputs may be any that keep to these rules, and one draw needn't show every extreme that they name: `pattern`: offset v of query block b names key block (b + 1 + v) mod 16; the 2 offsets of one query block and clip differ. Among the 6 clips of one dp index, one query block names one key block in at most 2 clips. `drop_flags`: 1 marks a layer dropped for a clip.
All inputs are finite; a program needn't handle non-finite values. No bound on the sum of `drop_flags` on one device may be relied on, other than what follows from the above.
Results may differ from a plain program's by a relative error of at most 0.0019.
Values may be sent and summed in bfloat16 or wider, within the bound.
No kernel may reach another device: no remote copies, remote signals or barrier semaphores. Data moves between devices by JAX's collectives and lax.ppermute only.
A program may use at most 64 MiB of HBM per device.

v0:
```python
import jax
import jax.numpy as jnp
from jax import lax
from jax.sharding import PartitionSpec as P

HEAD_DIM = 88
drop_rate = 0.25


def from_behind(x, axis, by):
    count = lax.axis_size(axis)
    return lax.ppermute(x, axis, [(i, (i + by) % count) for i in range(count)])


def body(
    resid_in,
    ln_gain,
    ln_bias,
    qkv_weight,
    q_bias,
    v_bias,
    out_weight,
    out_bias,
    pattern,
    drop_flags,
):
    clip_count = resid_in.shape[1]
    block_len = resid_in.shape[2]
    model_width = resid_in.shape[3]
    hidden = q_bias.shape[1]
    head_dim = HEAD_DIM
    head_count = hidden // head_dim
    listed_count = pattern.shape[2]
    tm_size = lax.axis_size("tm")
    my_block = lax.axis_index("tm")
    row_count = clip_count * block_len
    residual = resid_in[0].reshape(row_count, model_width)
    average = jnp.mean(residual, axis=1, keepdims=True)
    centred = residual - average
    spread = jnp.mean(centred * centred, axis=1, keepdims=True)
    normed = (centred * lax.rsqrt(spread + 1e-06) * ln_gain[0] + ln_bias[0]).astype(jnp.bfloat16)
    bias_full = jnp.concatenate([q_bias[0], jnp.zeros((hidden,), jnp.float32), v_bias[0]])
    projected_wide = jnp.dot(
        normed,
        lax.all_gather(qkv_weight[0], "dp", axis=1, tiled=True),
        preferred_element_type=jnp.float32,
    )
    projected = (projected_wide + bias_full).astype(jnp.bfloat16)
    queries = projected[:, :hidden].reshape(clip_count, block_len, head_count, head_dim)
    kv_local = projected[:, hidden:].reshape(clip_count, block_len, 2 * hidden)
    whole_pattern = lax.all_gather(pattern, "tm", axis=0, tiled=True)
    block_ids = jnp.arange(tm_size, dtype=jnp.int32)
    targets = (block_ids[:, None, None] + 1 + whole_pattern) % tm_size
    listed = jnp.sum((targets[..., None] == block_ids).astype(jnp.int32), axis=2)
    rank_table = jnp.cumsum(listed, axis=1) - listed
    capacity = max(2, (clip_count * listed_count + tm_size - 3) // (tm_size - 1))
    slot_ids = jnp.arange(capacity, dtype=jnp.int32)
    listed_mine = lax.dynamic_index_in_dim(listed, my_block, 2, keepdims=False)
    ranks_mine = lax.dynamic_index_in_dim(rank_table, my_block, 2, keepdims=False)
    selection = (
        (listed_mine[:, None, :] == 1) & (ranks_mine[:, None, :] == slot_ids[None, :, None])
    ).astype(jnp.bfloat16)
    outgoing = jnp.einsum(
        "qjc,cre->qjre", selection, kv_local, preferred_element_type=jnp.float32
    ).astype(jnp.bfloat16)
    incoming = lax.all_to_all(outgoing, "tm", split_axis=0, concat_axis=0, tiled=True)
    my_targets = lax.dynamic_index_in_dim(targets, my_block, 0, keepdims=False)
    my_ranks = lax.dynamic_index_in_dim(rank_table, my_block, 0, keepdims=False)
    slot_of = jnp.take_along_axis(my_ranks, my_targets, axis=1)
    flat_index = my_targets * capacity + slot_of
    remote = incoming.reshape(tm_size * capacity, block_len, 2 * hidden)[flat_index]
    gathered = jnp.concatenate([kv_local[:, None], remote], axis=1)
    gathered = gathered.reshape(clip_count, (1 + listed_count) * block_len, 2 * hidden)
    near_keys = gathered[..., :hidden].reshape(
        clip_count, (1 + listed_count) * block_len, head_count, head_dim
    )
    near_vals = gathered[..., hidden:].reshape(
        clip_count, (1 + listed_count) * block_len, head_count, head_dim
    )
    scores = jnp.einsum(
        "cqhd,ckhd->chqk", queries, near_keys, preferred_element_type=jnp.float32
    ) * head_dim ** (-0.5)
    weights = jnp.exp(scores)
    totals = jnp.sum(weights, axis=3)
    weighted = jnp.einsum(
        "chqk,ckhd->cqhd",
        weights.astype(jnp.bfloat16),
        near_vals,
        preferred_element_type=jnp.float32,
    )
    attended = (weighted / jnp.transpose(totals, (0, 2, 1))[..., None]).astype(jnp.bfloat16)
    attended = attended.reshape(row_count, hidden)
    branch = lax.dot_general(
        attended,
        lax.all_gather(out_weight[0], "dp", axis=1, tiled=True),
        (((1,), (1,)), ((), ())),
        preferred_element_type=jnp.float32,
    )
    branch = branch + out_bias[0]
    survive = (1 - drop_flags[0]).astype(jnp.float32)
    updated = residual.reshape(clip_count, block_len, model_width) + survive[
        :, None, None
    ] * branch.reshape(clip_count, block_len, model_width) / (1.0 - drop_rate)
    received = from_behind(updated, "pipe", 1)
    return received[None]


def solution(mesh):
    return jax.shard_map(
        body,
        mesh=mesh,
        in_specs=(
            P("pipe", "dp", "tm", None),
            P("pipe", None),
            P("pipe", None),
            P("pipe", None, "dp"),
            P("pipe", None),
            P("pipe", None),
            P("pipe", None, "dp"),
            P("pipe", None),
            P("tm", "dp", None),
            P("pipe", "dp"),
        ),
        out_specs=P("pipe", "dp", "tm", None),
        check_vma=False,
    )
```

profile of v0, /device:TPU:83, one launch (start us, length us, event | category | flops | bytes accessed | tf_op | source)
XLA Modules:
  0.0 681.6 jit_solution(11258215063038829731)
XLA Ops:
  6.5 0.0 all-gather.5.cloned.1.call-start
  6.5 2.6 copy.84
  9.1 0.0 all-gather.5.cloned.1.call-update
  9.1 0.7 reduce.3
  9.9 0.7 reduce.2
  10.6 0.0 copy-start.5
  10.6 0.0 copy-start.6
  10.6 0.0 copy-start.7
  10.6 1.8 reduce_sum.36
  12.4 0.1 div.23
  12.5 0.0 copy-done
  12.5 0.3 multiply_reduce_fusion
  12.9 0.1 rsqrt.12
  12.9 0.0 copy-done.5
  13.0 0.0 copy-done.6
  13.0 44.7 %all_gather.10 = s32[16,6,2]{1,2,0:T(2,128)S(1)} all-gather(s32[1,6,2]{1,2,0:T(2,128)S(1)} %copy-done.7), channel_id=1, replica_groups=mesh['tm'=16,'pipe'=2,'dp'=16] {'tm'}, dimensions={0}, use_global_device_ids=true | all-gather | bytes 816 | tf_op jit(solution)/shard_map/all_gather | solution.py:51
  57.7 0.1 and_select_fusion
  57.8 0.1 copy.86
  57.9 0.1 concatenate.6
  58.0 0.1 convert_reduce_fusion
  58.1 0.2 reduce-window_subtract_fusion
  58.3 0.2 dynamic-slice_reduce_fusion
  58.5 0.3 fusion.27
  58.8 0.4 fusion.14
  59.2 214.3 %all-gather.5.cloned.1.call-done = bf16[1,1408,2112]{1,0,2:T(2,128)(2,1)} async-done(((bf16[1,1408,132]{1,0,2:T(2,128)(2,1)}), bf16[1,1408,2112]{1,0,2:T(2,128)(2,1)}) %all-gather.5.cloned.1.call-update) | async-done | bytes 5947408 | tf_op jit(solution)/shard_map/all_gather | solution.py:45
  273.5 7.8 %fusion.6 = bf16[384,2112]{0,1:T(8,128)(2,1)S(1)} fusion(bf16[384,1408]{1,0:T(8,128)(2,1)S(1)} %fusion.14, bf16[1,1408,2112]{1,0,2:T(2,128)(2,1)} %all-gather.5.cloned.1.call-done, f32[2112]{0:T(1024)S(1)} %concatenate.6), kind=kOutput, calls=%fused_computation.7 | convolution fusion | flops 2285420544 | bytes 8659200 | tf_op jit(solution)/shard_map/dot_general | solution.py:43
  281.3 0.0 copy-start.2
  281.3 1.1 copy-done.2
  282.4 1.1 slice.20
  283.5 1.7 copy.85
  285.2 2.3 convolution_convert_fusion
  287.6 3.9 copy.89
  291.4 12.0 %all-to-all-start = ((bf16[16,2,64,1408]{3,2,1,0:T(8,128)(2,1)}), bf16[16,2,64,1408]{3,2,1,0:T(8,128)(2,1)}, u32[]{:S(2)}, u32[]{:S(2)}) async-start(bf16[16,2,64,1408]{3,2,1,0:T(8,128)(2,1)} %copy.89), calls=%async_computation | async-start | bytes 11534336 | tf_op jit(solution)/shard_map/all_to_all | solution.py:66
  303.5 0.2 all-gather.7.cloned.1.call-start
  303.7 0.0 copy-done.3
  303.7 0.9 copy.99
  304.6 0.0 all-gather.7.cloned.1.call-update
  304.6 0.0 copy-start.4
  304.6 0.0 copy-start.8
  304.7 0.1 copy.90
  304.8 0.1 reshape.187
  304.9 0.7 gather_fusion.1
  305.5 0.1 gather.10
  305.6 0.1 copy.91
  305.7 0.1 copy.92
  305.8 0.1 reshape.181
  306.0 1.9 slice.22
  307.9 2.7 reshape.199
  310.6 328.4 %all-to-all-done = bf16[16,2,64,1408]{3,2,1,0:T(8,128)(2,1)} async-done(((bf16[16,2,64,1408]{3,2,1,0:T(8,128)(2,1)}), bf16[16,2,64,1408]{3,2,1,0:T(8,128)(2,1)}, u32[]{:S(2)}, u32[]{:S(2)}) %all-to-all-start) | async-done | bytes 5767200 | tf_op jit(solution)/shard_map/all_to_all | solution.py:66
  639.0 4.9 gather_fusion
  643.9 1.9 pad_maximum_fusion
  645.8 2.6 fusion.36
  648.4 3.9 copy.94
  652.3 4.0 copy.96
  656.3 3.5 fusion.9
  659.8 0.8 fusion.19
  660.6 0.5 copy.98
  661.1 0.6 reshape.177
  661.7 0.0 all-gather.7.cloned.1.call-done
  661.7 3.2 convolution_add_fusion
  664.9 0.4 bitcast_add_fusion
  665.4 4.2 collective-permute-start
  669.5 3.9 collective-permute-done
  673.4 1.3 copy.129
  (20 shorter events, 0.1 us)
Async XLA Ops:
  6.5 6.0 copy-start
  6.5 266.9 %all-gather.5.cloned.1.call-start = ((), (), s32[]{:S(2)}) async-start(), calls=%async_computation.1 | async-start | bytes 12638208 | tf_op jit(solution)/shard_map/all_gather | solution.py:45
  10.6 2.4 copy-start.5
  10.6 2.4 copy-start.6
  10.6 2.4 copy-start.7
  281.3 1.2 copy-start.2
  291.4 12.3 %copy-start.3 = (bf16[1,1408,44]{1,2,0:T(8,128)(2,1)S(1)}, bf16[1,1408,44]{1,2,0:T(8,128)(2,1)}, u32[]{:S(2)}) copy-start(bf16[1,1408,44]{1,2,0:T(8,128)(2,1)} %param.16) | copy-start | bytes 371716
  291.4 347.6 %all-to-all-start = ((bf16[16,2,64,1408]{3,2,1,0:T(8,128)(2,1)}), bf16[16,2,64,1408]{3,2,1,0:T(8,128)(2,1)}, u32[]{:S(2)}, u32[]{:S(2)}) async-start(bf16[16,2,64,1408]{3,2,1,0:T(8,128)(2,1)} %copy.89), calls=%async_computation | async-start | bytes 11534336 | tf_op jit(solution)/shard_map/all_to_all | solution.py:66
  303.5 358.2 %all-gather.7.cloned.1.call-start = ((), (), s32[]{:S(2)}) async-start(), calls=%async_computation.2 | async-start | bytes 4212736 | tf_op jit(solution)/shard_map/all_gather | solution.py:95
  304.6 1.3 copy-start.4
  304.6 1.3 copy-start.8
  656.3 3.5 copy-start.1
  665.4 8.0 %collective-permute-start = (f32[6,64,1408]{2,1,0:T(8,128)S(1)}, f32[6,64,1408]{2,1,0:T(8,128)S(1)}, u32[]{:S(2)}, u32[]{:S(2)}) collective-permute-start(f32[6,64,1408]{2,1,0:T(8,128)S(1)} %bitcast_add_fusion), channel_id=1, source_target_pairs={{0,16},{16,0},{1,17},{17,1},{2,18},{18,2},{3,19},{19,3},{4,20},{20... | collective-permute-start | bytes 6488072 | tf_op jit(solution)/shard_map/ppermute | solution.py:12
Sparse Core Ops, SparseCore 0:
  9.4 264.0 all-gather.4
  306.4 311.5 all-gather.6
where the time goes:
time: 682 us
  waiting for transfers between devices  547 us (80%)
  blocking collectives  44.7 us (7%)
  local copies, waits for them, and re-layouts  35.5 us (5%)
  matrix products  17.6 us (3%)
  starting transfers between devices  16.4 us (2%)
  between operations  13.7 us (2%)
  other arithmetic  7.06 us (1%)
    all_to_all x1, waiting for transfers between devices, body(): lax.all_to_all(outgoing, 'tm', split_axis=0, concat_axis=0, tiled=True)  328 us
    all_gather x1, waiting for transfers between devices, body(): lax.all_gather(qkv_weight[0], 'dp', axis=1, tiled=True)  214 us
    all_gather x1, blocking collectives, body(): whole_pattern = lax.all_gather(pattern, 'tm', axis=0, tiled=True)  44.7 us
  transfers between devices with their start and end apart: 4, of which 3 were waited for; matrix products, arithmetic and copies ran while one was open for 5% of the time, Pallas kernels for 0%

commit v1 on v0

--- a/solution.py
+++ b/solution.py
@@ -42,7 +42,9 @@
     bias_full = jnp.concatenate([q_bias[0], jnp.zeros((hidden,), jnp.float32), v_bias[0]])
     projected_wide = jnp.dot(
         normed,
-        lax.all_gather(qkv_weight[0], "dp", axis=1, tiled=True),
+        jnp.concatenate(
+            lax.all_to_all(jnp.stack([qkv_weight[0]] * lax.axis_size("dp")), "dp", 0, 0), axis=1
+        ),
         preferred_element_type=jnp.float32,
     )
     projected = (projected_wide + bias_full).astype(jnp.bfloat16)

time: 682 us -> 573 us (0.84)
  waiting for transfers between devices: 547 us -> 301 us
  blocking collectives: 44.7 us -> 165 us
  starting transfers between devices: 16.4 us -> 27.4 us
  local copies, waits for them, and re-layouts: 35.5 us -> 44.9 us
    all_gather x1 -> x0, waiting for transfers between devices: 214 us -> none  [body(): lax.all_gather(qkv_weight[0], 'dp', axis=1, tiled=True)]
    all_gather x1, blocking collectives: 44.7 us -> 165 us  [body(): whole_pattern = lax.all_gather(pattern, 'tm', axis=0, tiled=True)]
    all_to_all x1, waiting for transfers between devices: 328 us -> 297 us  [body(): lax.all_to_all(outgoing, 'tm', split_axis=0, concat_axis=0, tiled=True)]
    reshape x0 -> x1, local copies, waits for them, and re-layouts: none -> 8.07 us  [body(): jnp.concatenate(lax.all_to_all(jnp.stack([qkv_weight[0]] * lax.axis_size(...]
    all_to_all x0 -> x1, starting transfers between devices: none -> 7.58 us  [body(): lax.all_to_all(jnp.stack([qkv_weight[0]] * lax.axis_size('dp')), 'dp', 0, 0)]
  transfers between devices with their start and end apart: 4 -> 4, of which waited for: 3 -> 2; matrix products, arithmetic and copies ran while one was open for 5% -> 6% of each run, Pallas kernels for 0% -> 0%
where the time goes in v1:
time: 573 us; the launch traced here: 572 us
  waiting for transfers between devices  301 us (53%)
  blocking collectives  165 us (29%)
  local copies, waits for them, and re-layouts  44.9 us (8%)
  starting transfers between devices  27.4 us (5%)
  matrix products  15.9 us (3%)
  between operations  13.7 us (2%)
    all_to_all x1, waiting for transfers between devices, body(): lax.all_to_all(outgoing, 'tm', split_axis=0, concat_axis=0, tiled=True)  297 us
    all_gather x1, blocking collectives, body(): whole_pattern = lax.all_gather(pattern, 'tm', axis=0, tiled=True)  165 us
    all_to_all x1, starting transfers between devices, body(): lax.all_to_all(outgoing, 'tm', split_axis=0, concat_axis=0, tiled=True)  17.2 us
  transfers between devices with their start and end apart: 4, of which 2 were waited for; matrix products, arithmetic and copies ran while one was open for 6% of the time, Pallas kernels for 0%

profile of v1, /device:TPU:83, one launch (start us, length us, event | category | flops | bytes accessed | tf_op | source)
XLA Modules:
  0.0 572.3 jit_solution(12624082161876811554)
XLA Ops:
  6.5 4.0 stack.3
  10.6 0.0 copy-start.8
  10.6 0.0 copy-start
  10.6 7.6 %all-to-all-start = ((bf16[16,1408,132]{1,2,0:T(8,128)(2,1)}), bf16[16,1408,132]{1,2,0:T(8,128)(2,1)}, u32[]{:S(2)}, u32[]{:S(2)}) async-start(bf16[16,1408,132]{1,2,0:T(8,128)(2,1)} %stack.3), calls=%async_computation | async-start | bytes 12255232 | tf_op jit(solution)/shard_map/all_to_all | solution.py:46
  18.2 0.0 copy-done.9
  18.2 165.1 %all_gather.6 = s32[16,6,2]{1,2,0:T(2,128)S(1)} all-gather(s32[1,6,2]{1,2,0:T(2,128)S(1)} %copy-done.9), channel_id=1, replica_groups=mesh['tm'=16,'pipe'=2,'dp'=16] {'tm'}, dimensions={0}, use_global_device_ids=true | all-gather | bytes 816 | tf_op jit(solution)/shard_map/all_gather | solution.py:53
  183.3 0.1 and_select_fusion
  183.4 0.1 copy.83
  183.5 0.0 copy-done.4
  183.6 0.0 copy-done.5
  183.6 0.0 copy-done.7
  183.6 0.0 copy-done.8
  183.7 0.0 copy-done
  183.7 0.2 reduce_sum.36
  183.9 0.1 concatenate.6
  183.9 0.1 convert_reduce_fusion
  184.0 0.2 reduce-window_subtract_fusion
  184.2 0.2 dynamic-slice_reduce_fusion
  184.4 0.3 fusion.15
  184.7 0.3 multiply_reduce_fusion
  185.1 0.4 add_convert_fusion
  185.5 0.0 all-to-all-done
  185.5 8.1 %reshape.195 = bf16[1408,2112]{0,1:T(8,128)(2,1)} reshape(bf16[1408,16,132]{0,2,1:T(8,128)(2,1)} %bitcast.4) | data formatting | bytes 11894784 | tf_op jit(solution)/shard_map/reshape | solution.py:45
  193.6 6.1 %fusion = bf16[384,2112]{0,1:T(8,128)(2,1)S(1)} fusion(bf16[384,1408]{1,0:T(8,128)(2,1)S(1)} %bitcast.73, bf16[1408,2112]{0,1:T(8,128)(2,1)} %reshape.195, f32[2112]{0:T(1024)S(1)} %concatenate.6), kind=kOutput, calls=%fused_computation.4 | convolution fusion | flops 2285420544 | bytes 8659200 | tf_op jit(solution)/shard_map/dot_general | solution.py:43
  199.7 0.0 copy-start.2
  199.7 1.1 copy-done.2
  200.9 1.1 slice.20
  202.0 1.7 copy.82
  203.7 2.3 convolution_convert_fusion
  206.0 3.9 copy.86
  209.9 17.2 %all-to-all-start.1 = ((bf16[16,2,64,1408]{3,2,1,0:T(8,128)(2,1)}), bf16[16,2,64,1408]{3,2,1,0:T(8,128)(2,1)}, u32[]{:S(2)}, u32[]{:S(2)}) async-start(bf16[16,2,64,1408]{3,2,1,0:T(8,128)(2,1)} %copy.86), calls=%async_computation.1 | async-start | bytes 11534336 | tf_op jit(solution)/shard_map/all_to_all | solution.py:68
  227.0 0.2 all-gather.3.cloned.1.call-start
  227.3 0.0 copy-done.3
  227.3 0.9 copy.96
  228.1 0.0 all-gather.3.cloned.1.call-update
  228.2 0.0 copy-start.6
  228.2 0.0 copy-start.10
  228.2 0.1 copy.87
  228.3 0.1 reshape.212
  228.4 0.7 gather_fusion.1
  229.1 0.1 gather.10
  229.2 0.1 copy.88
  229.3 0.1 copy.89
  229.4 0.1 reshape.206
  229.5 0.0 copy-done.6
  229.5 0.0 copy-done.10
  229.5 1.9 slice.22
  231.5 2.7 reshape.223
  234.1 297.3 %all-to-all-done.1 = bf16[16,2,64,1408]{3,2,1,0:T(8,128)(2,1)} async-done(((bf16[16,2,64,1408]{3,2,1,0:T(8,128)(2,1)}), bf16[16,2,64,1408]{3,2,1,0:T(8,128)(2,1)}, u32[]{:S(2)}, u32[]{:S(2)}) %all-to-all-start.1) | async-done | bytes 5767200 | tf_op jit(solution)/shard_map/all_to_all | solution.py:68
  531.4 4.9 gather_fusion
  536.3 1.9 pad_maximum_fusion
  538.2 2.6 fusion.24
  540.9 4.0 copy.93
  544.8 3.9 copy.91
  548.8 3.5 fusion.1
  552.3 0.8 fusion.7
  553.0 0.5 copy.95
  553.6 0.6 reshape.202
  554.1 0.0 all-gather.3.cloned.1.call-done
  554.2 3.2 convolution_add_fusion.1
  557.4 0.4 bitcast_add_fusion
  557.8 2.5 collective-permute-start
  560.3 3.9 collective-permute-done
  564.1 1.3 copy.117
  (22 shorter events, 0.2 us)
Async XLA Ops:
  10.6 7.6 %copy-start.9 = (s32[1,6,2]{1,2,0:T(2,128)S(1)}, s32[1,6,2]{1,2,0:T(2,128)}, u32[]{:S(2)}) copy-start(s32[1,6,2]{1,2,0:T(2,128)} %param.18) | copy-start | bytes 148
  10.6 173.0 %copy-start.4 = (f32[1,1408]{1,0:T(1,128)S(1)}, f32[1,1408]{1,0:T(1,128)}, u32[]{:S(2)}) copy-start(f32[1,1408]{1,0:T(1,128)} %param.11) | copy-start | bytes 16900
  10.6 173.0 %copy-start.5 = (f32[1,1408]{1,0:T(1,128)S(1)}, f32[1,1408]{1,0:T(1,128)}, u32[]{:S(2)}) copy-start(f32[1,1408]{1,0:T(1,128)} %param.12) | copy-start | bytes 16900
  10.6 173.0 %copy-start.7 = (f32[1,704]{1,0:T(1,128)S(1)}, f32[1,704]{1,0:T(1,128)}, u32[]{:S(2)}) copy-start(f32[1,704]{1,0:T(1,128)} %param.14) | copy-start | bytes 8452
  10.6 173.1 %copy-start.8 = (f32[1,704]{1,0:T(1,128)S(1)}, f32[1,704]{1,0:T(1,128)}, u32[]{:S(2)}) copy-start(f32[1,704]{1,0:T(1,128)} %param.15) | copy-start | bytes 8452
  10.6 173.1 %copy-start = (f32[1,6,64,1408]{3,2,1,0:T(8,128)S(1)}, f32[1,6,64,1408]{3,2,1,0:T(8,128)}, u32[]{:S(2)}) copy-start(f32[1,6,64,1408]{3,2,1,0:T(8,128)} %param.10) | copy-start | bytes 6488068
  10.6 174.9 %all-to-all-start = ((bf16[16,1408,132]{1,2,0:T(8,128)(2,1)}), bf16[16,1408,132]{1,2,0:T(8,128)(2,1)}, u32[]{:S(2)}, u32[]{:S(2)}) async-start(bf16[16,1408,132]{1,2,0:T(8,128)(2,1)} %stack.3), calls=%async_computation | async-start | bytes 12255232 | tf_op jit(solution)/shard_map/all_to_all | solution.py:46
  199.7 1.2 copy-start.2
  209.9 17.4 %copy-start.3 = (bf16[1,1408,44]{1,2,0:T(8,128)(2,1)S(1)}, bf16[1,1408,44]{1,2,0:T(8,128)(2,1)}, u32[]{:S(2)}) copy-start(bf16[1,1408,44]{1,2,0:T(8,128)(2,1)} %param.16) | copy-start | bytes 371716
  209.9 321.6 %all-to-all-start.1 = ((bf16[16,2,64,1408]{3,2,1,0:T(8,128)(2,1)}), bf16[16,2,64,1408]{3,2,1,0:T(8,128)(2,1)}, u32[]{:S(2)}, u32[]{:S(2)}) async-start(bf16[16,2,64,1408]{3,2,1,0:T(8,128)(2,1)} %copy.86), calls=%async_computation.1 | async-start | bytes 11534336 | tf_op jit(solution)/shard_map/all_to_all | solution.py:68
  227.0 327.1 %all-gather.3.cloned.1.call-start = ((), (), s32[]{:S(2)}) async-start(), calls=%async_computation.2 | async-start | bytes 4212736 | tf_op jit(solution)/shard_map/all_gather | solution.py:97
  228.2 1.3 copy-start.6
  228.2 1.3 copy-start.10
  548.8 3.5 copy-start.1
  557.8 6.3 %collective-permute-start = (f32[6,64,1408]{2,1,0:T(8,128)S(1)}, f32[6,64,1408]{2,1,0:T(8,128)S(1)}, u32[]{:S(2)}, u32[]{:S(2)}) collective-permute-start(f32[6,64,1408]{2,1,0:T(8,128)S(1)} %bitcast_add_fusion), channel_id=1, source_target_pairs={{0,16},{16,0},{1,17},{17,1},{2,18},{18,2},{3,19},{19,3},{4,20},{20... | collective-permute-start | bytes 6488072 | tf_op jit(solution)/shard_map/ppermute | solution.py:12
Sparse Core Ops, SparseCore 0:
  229.9 263.1 all-gather.2
